TPU v7x, 32 devices: a whole 2x2x4 slice. The times are simulated.
32 devices in a mesh: ctx: 8 (over z, core), tp: 4 (over y, x).
Axes of the slice: x: 2, y: 2, z: 4, core: 2. Of those that a mesh axis runs over, the one named last changes fastest.
Arguments:
- tokens: bfloat16 [2048, 4096], P('ctx', 'tp'), may hold values from -6 to 6
- w_z: bfloat16 [4096, 2048], P(None, 'tp'), may hold values from -0.09375 to 0.09375
- w_x: bfloat16 [4096, 2048], P(None, 'tp'), may hold values from -0.09375 to 0.09375
- w_bc: bfloat16 [4096, 512], P(None, 'tp'), may hold values from -0.09375 to 0.09375
- conv_x: float32 [4, 2048], P(None, 'tp'), may hold values from -3 to 3
- conv_bc: float32 [4, 512], P(None, 'tp'), may hold values from -3 to 3
- bias_x: float32 [2048], P('tp'), may hold values from -0.5 to 0.5
- bias_bc: float32 [512], P('tp'), may hold values from -0.5 to 0.5
- decay_logarithm: float32 [2048, 32], P('ctx', 'tp'), may hold values from -1.3 to 0, as said below
- head_step: float32 [32], P('tp'), may hold values from 0 to 0.3, as said below
- skip: float32 [32], P('tp'), may hold values from 0.5 to 1.5
- gain: float32 [2048], P('tp'), may hold values from 0.5 to 1.5
Outputs:
- normed: bfloat16 [2048, 2048], P('ctx', 'tp')
Inputs may be any that keep to these rules, and one draw needn't show every extreme that they name: decay_logarithm is negative. head_step is positive.
All inputs are finite; a program needn't handle non-finite values.
Results may differ from a plain program's by a relative error of at most 0.0095.
Values may be sent and summed in bfloat16 or wider, within the bound.
No kernel may reach another device: no remote copies, remote signals or barrier semaphores. Data moves between devices by JAX's collectives and lax.ppermute only.
A program may use at most 64 MiB of HBM per device.

v0:
```python
import jax
import jax.numpy as jnp
from jax import lax
from jax.sharding import PartitionSpec as P

KERNEL = 4
STRETCH = 256


def shifted(block, axis, distance):
    devices = range(lax.axis_size(axis))
    route = [(i - distance, i) for i in devices if i - distance in devices]
    return lax.ppermute(block, axis, route)


def partner(value, axis, distance):
    mask = 2**distance
    pairs = [(source, source ^ mask) for source in range(lax.axis_size(axis))]
    return lax.ppermute(value, axis, pairs)


def carried_in(shard, axis, combine, identity):
    size, place = (lax.axis_size(axis), lax.axis_index(axis))
    everything = jax.tree.map(lambda part: lax.all_gather(part, axis), shard)
    start = jax.tree.map(
        lambda part, zero: jnp.broadcast_to(jnp.asarray(zero, part.dtype), part.shape),
        shard,
        identity,
    )

    def lap(k, before):
        reached = k < place
        new = combine(before, jax.tree.map(lambda part: part[k], everything))
        return jax.tree.map(lambda a, b: jnp.where(reached, a, b), new, before)

    return lax.fori_loop(0, size, lap, start)


def state_combine(earlier, later):
    return (earlier[0] + later[0], jnp.exp(later[0])[:, None, None] * earlier[1] + later[1])


def local(
    tokens, w_z, w_x, w_bc, conv_x, conv_bc, bias_x, bias_bc, decay_logarithm, head_step, skip, gain
):
    tok_rows = tokens.shape[0]
    x_width = w_x.shape[1]
    bc_width = w_bc.shape[1]
    heads_local = head_step.shape[0]
    head_dim = x_width // heads_local
    gathered = lax.all_gather(tokens, "tp", axis=1, tiled=True)
    gate_sum = jnp.dot(gathered, w_z, preferred_element_type=jnp.float32)
    x_sum = jnp.dot(gathered, w_x, preferred_element_type=jnp.float32)
    bc_sum = jnp.dot(gathered, w_bc, preferred_element_type=jnp.float32)
    gate_in = gate_sum.astype(jnp.bfloat16)
    x_pre = x_sum.astype(jnp.bfloat16)
    bc_pre = bc_sum.astype(jnp.bfloat16)
    pre_conv = jnp.concatenate([x_pre, bc_pre], axis=1)
    rim_rows = shifted(pre_conv[tok_rows - (KERNEL - 1) :], "ctx", 1)
    extended = jnp.concatenate([rim_rows, pre_conv], axis=0).astype(jnp.float32)
    conv_taps = jnp.concatenate([conv_x, conv_bc], axis=1)
    conv_bias = jnp.concatenate([bias_x, bias_bc], axis=0)
    conv_total = conv_bias[None, :] + jnp.zeros((tok_rows, x_width + bc_width), jnp.float32)
    for offset in range(KERNEL):
        conv_total = conv_total + conv_taps[offset][None, :] * extended[offset : offset + tok_rows]
    conv_out = jax.nn.silu(conv_total).astype(jnp.bfloat16)
    x_conv = conv_out[:, :x_width]
    own_bc = conv_out[:, x_width:]
    other_bc = partner(own_bc, "tp", 0)
    holds_b = lax.axis_index("tp") % 2 == 0
    b_proj = jnp.where(holds_b, own_bc, other_bc)
    c_proj = jnp.where(holds_b, other_bc, own_bc)
    stretch_len = STRETCH
    stretch_count = tok_rows // stretch_len
    x_float = x_conv.astype(jnp.float32).reshape(stretch_count, stretch_len, heads_local, head_dim)
    cum_decay = jnp.cumsum(decay_logarithm.reshape(stretch_count, stretch_len, heads_local), axis=1)
    b_stretches = b_proj.reshape(stretch_count, stretch_len, bc_width)
    c_stretches = c_proj.reshape(stretch_count, stretch_len, bc_width)
    scores = jnp.einsum(
        "cin,cjn->cij", c_stretches, b_stretches, preferred_element_type=jnp.float32
    )
    causal = jnp.tril(jnp.ones((stretch_len, stretch_len), dtype=bool))[None, :, :, None]
    pair_diff = cum_decay[:, :, None, :] - cum_decay[:, None, :, :]
    segment = jnp.where(causal, jnp.exp(jnp.where(causal, pair_diff, 0.0)), 0.0)
    mixing = segment * scores[:, :, :, None] * head_step
    intra_out = jnp.einsum("cijh,cjhp->cihp", mixing, x_float, precision=lax.Precision.HIGHEST)
    b_float = b_stretches.astype(jnp.float32)
    c_float = c_stretches.astype(jnp.float32)
    end_weight = jnp.exp(cum_decay[:, -1:, :] - cum_decay) * head_step
    stretch_states = jnp.einsum(
        "cjh,cjhp,cjn->chpn", end_weight, x_float, b_float, precision=lax.Precision.HIGHEST
    )
    stretch_decay = cum_decay[:, -1, :]

    def advance(state, item):
        added, decay_sum = item
        return (jnp.exp(decay_sum)[:, None, None] * state + added, state)

    zero_state = jnp.zeros((heads_local, head_dim, bc_width), jnp.float32)
    section_final_state, prior_section_state = lax.scan(
        advance, zero_state, (stretch_states, stretch_decay)
    )
    total_decay = jnp.sum(stretch_decay, axis=0)
    _, incoming = carried_in(
        (total_decay, section_final_state),
        "ctx",
        state_combine,
        (jnp.zeros_like(total_decay), zero_state),
    )
    prefix_decay = jnp.cumsum(stretch_decay, axis=0) - stretch_decay
    entering = prior_section_state + jnp.exp(prefix_decay)[:, :, None, None] * incoming[None]
    inter_out = (
        jnp.einsum("cin,chpn->cihp", c_float, entering, precision=lax.Precision.HIGHEST)
        * jnp.exp(cum_decay)[:, :, :, None]
    )
    head_out = (intra_out + inter_out).reshape(tok_rows, heads_local, head_dim)
    head_out = head_out + skip[None, :, None] * x_conv.astype(jnp.float32).reshape(
        tok_rows, heads_local, head_dim
    )
    gated = head_out.reshape(tok_rows, x_width) * jax.nn.silu(gate_in.astype(jnp.float32))
    local_square = jnp.sum(gated * gated, axis=1)
    other_square = partner(local_square, "tp", 0)
    mean_square = (local_square + other_square) / (2 * x_width)
    scaled = gated * lax.rsqrt(mean_square + 1e-05)[:, None]
    return (scaled * gain[None, :]).astype(jnp.bfloat16)


def solution(mesh):
    in_specs = (
        P("ctx", "tp"),
        P(None, "tp"),
        P(None, "tp"),
        P(None, "tp"),
        P(None, "tp"),
        P(None, "tp"),
        P("tp"),
        P("tp"),
        P("ctx", "tp"),
        P("tp"),
        P("tp"),
        P("tp"),
    )
    out_specs = P("ctx", "tp")
    return jax.shard_map(local, mesh=mesh, in_specs=in_specs, out_specs=out_specs, check_vma=False)
```

profile of v0, /device:TPU:0, one launch (start us, length us, event | category | flops | bytes accessed | tf_op | source)
XLA Modules:
  0.0 117.3 jit_solution(2576824456044173264)
XLA Ops:
  6.5 0.7 all-gather.5.cloned.1.call-update
  7.3 0.0 all-gather.7.cloned.1.call-start
  7.3 1.3 %reduce-window.6 = f32[1,8,2,128]{3,1,2,0:T(8,128)S(1)} reduce-window(f32[1,8,2,128]{3,1,2,0:T(8,128)} %bitcast.71, f32[]{:T(128)} %constant.69.clone.1), window={size=1x1x1x128 pad=0_0x0_0x0_0x127_0}, to_apply=%region_0.1 | reduce-window | flops 260096 | bytes 16388 | tf_op jit(solution)/shard_map/reduce-window
  8.6 0.2 slice_reduce_fusion
  8.8 0.7 constant_dynamic-update-slice_fusion.1
  9.5 0.7 constant_dynamic-update-slice_fusion
  10.2 0.1 exponential_bitcast_fusion.1
  10.3 0.2 slice_reduce_fusion.5
  10.4 0.7 multiply_bitcast_fusion
  11.2 35.9 %all-gather.5.cloned.1.call-done = bf16[256,4096]{1,0:T(8,128)(2,1)} async-done(((bf16[256,1024]{1,0:T(8,128)(2,1)}), bf16[256,4096]{1,0:T(8,128)(2,1)}) %all-gather.5.cloned.1.call-update) | async-done | bytes 2097168 | tf_op jit(solution)/shard_map/all_gather | solution.py:51
  47.1 4.2 %convolution_convert_fusion.1 = bf16[256,512]{1,0:T(8,128)(2,1)S(1)} fusion(bf16[256,4096]{1,0:T(8,128)(2,1)} %all-gather.5.cloned.1.call-done, bf16[4096,512]{1,0:T(8,128)(2,1)} %param.16), kind=kOutput, calls=%fused_computation.16 | convolution fusion | flops 1073872896 | bytes 6553600 | tf_op jit(solution)/shard_map/dot_general | solution.py:53
  51.4 0.0 copy-start.3
  51.4 0.0 copy-start.6
  51.4 0.7 convolution_convert_fusion.2
  52.1 1.6 %collective-permute-start = (bf16[3,640]{1,0:T(4,128)(2,1)S(1)}, bf16[3,640]{1,0:T(4,128)(2,1)S(1)}, u32[]{:S(2)}, u32[]{:S(2)}) collective-permute-start(bf16[3,640]{1,0:T(4,128)(2,1)S(1)} %pad_maximum_fusion), channel_id=1, source_target_pairs={{0,4},{4,8},{8,12},{12,16},{16,20},{20,24},{24,28},{1,5},{5,9},{9,... | collective-permute-start | bytes 11528 | tf_op jit(solution)/shard_map/ppermute | solution.py:13
  53.7 0.8 collective-permute-done
  54.5 0.1 maximum_convert_fusion
  54.6 0.0 copy-start.4
  54.6 0.4 multiply_convert_fusion
  55.0 0.0 copy-start.5
  55.1 1.5 %collective-permute-start.1 = (bf16[256,128]{1,0:T(8,128)(2,1)S(1)}, bf16[256,128]{1,0:T(8,128)(2,1)S(1)}, u32[]{:S(2)}, u32[]{:S(2)}) collective-permute-start(bf16[256,128]{1,0:T(8,128)(2,1)S(1)} %slice.67), channel_id=1, source_target_pairs={{0,1},{1,0},{2,3},{3,2},{4,5},{5,4},{6,7},{7,6},{8,9},{9,8},{10,11... | collective-permute-start | bytes 196616 | tf_op jit(solution)/shard_map/ppermute | solution.py:19
  56.6 0.1 copy.28
  56.8 2.6 %collective-permute-done.1 = bf16[256,128]{1,0:T(8,128)(2,1)S(1)} collective-permute-done((bf16[256,128]{1,0:T(8,128)(2,1)S(1)}, bf16[256,128]{1,0:T(8,128)(2,1)S(1)}, u32[]{:S(2)}, u32[]{:S(2)}) %collective-permute-start.1) | collective-permute-done | bytes 65568 | tf_op jit(solution)/shard_map/ppermute | solution.py:19
  59.4 1.1 convolution_add_fusion
  60.5 0.0 all-gather.7.cloned.1.call-update
  60.5 0.1 copy.29
  60.6 0.1 mul.197
  60.7 0.1 mul.198
  60.8 14.2 %all-gather = f32[8,1,8]{2,1,0:T(1,128)S(1)} all-gather(f32[1,1,8]{2,1,0:T(1,128)S(1)} %copy.29), channel_id=2, replica_groups=mesh['ctx'=8,'tp'=4] {'ctx'}, dimensions={0}, use_global_device_ids=true | all-gather | bytes 288 | tf_op jit(solution)/shard_map/all_gather | solution.py:24
  75.0 0.1 fusion.32
  75.1 0.2 fusion.31
  75.3 1.8 %fusion.8 = f32[1,256,8,64]{1,3,2,0:T(8,128)S(1)} fusion(bf16[256,8,64]{0,2,1:T(8,128)(2,1)S(1)} %bitcast.69, f32[8]{0:T(128)S(1)} %copy-done.5, f32[256,256]{1,0:T(8,128)S(1)} %fusion.31, f32[256,8]{0,1:T(8,128)S(1)} %fusion.32, pred[256,256]{1,0:T(8,128)(4,1)S(1)} %iota_compare_fusion), kind=kOutput, calls=%fused_computation.10 | convolution fusion | flops 405274624 | bytes 1122336 | tf_op jit(solution)/shard_map/cijh,cjhp->cihp/dot_general | solution.py:86
  77.1 15.3 %all-gather.7.cloned.1.call-done = f32[64,64,128]{2,1,0:T(8,128)} async-done(((f32[8,64,128]{2,1,0:T(8,128)}), f32[64,64,128]{2,1,0:T(8,128)}) %all-gather.7.cloned.1.call-update) | async-done | bytes 2097168 | tf_op jit(solution)/shard_map/all_gather | solution.py:24
  92.4 8.7 %while.9 = (s32[]{:T(128)}, f32[8,64,128]{2,1,0:T(8,128)S(1)}, s32[]{:T(128)}, f32[8,8]{1,0:T(8,128)S(1)}, f32[8,8,64,128]{3,2,1,0:T(8,128)}, /*index=5*/s32[]{:T(128)}, s32[]{:T(128)}) while((s32[]{:T(128)}, f32[8,64,128]{2,1,0:T(8,128)S(1)}, s32[]{:T(128)}, f32[8,8]{1,0:T(8,128)S(1)}, f32[8,8,64,128]{3,2,1,0:T(8,128)}, ...), condition=%wide.region_3.4_spmd.clone, body=%wide.region_2.3_spmd.clone.sunk | while | flops 262148 | bytes 786633 | solution.py:36
  92.4 1.1 fusion.47
  93.5 1.1 fusion.47
  94.6 1.1 fusion.47
  95.7 1.1 fusion.47
  96.8 1.1 fusion.47
  97.8 1.1 fusion.47
  98.9 1.1 fusion.47
  100.0 1.1 fusion.47
  101.1 0.4 fusion.12
  101.5 0.2 copy.30
  101.7 4.3 %multiply_reduce_fusion = (f32[256]{0:T(256)S(1)}, f32[256,512]{1,0:T(8,128)S(1)}) fusion(bf16[256,4096]{1,0:T(8,128)(2,1)} %all-gather.5.cloned.1.call-done, bf16[4096,512]{1,0:T(8,128)(2,1)} %param.15, f32[256,512]{1,0:T(8,128)S(1)} %copy.30, bf16[256,640]{1,0:T(8,128)(2,1)S(1)} %multiply_convert_fusion, f32[512]{0:T(512)S(1)} %mul.198), kind=kOutput, calls=%fused_computation.35 | convolution fusion | flops 1075314432 | bytes 7605248 | tf_op jit(solution)/shard_map/dot_general | solution.py:52
  106.0 1.5 %collective-permute-start.2 = (f32[256]{0:T(256)S(1)}, f32[256]{0:T(256)S(1)}, u32[]{:S(2)}, u32[]{:S(2)}) collective-permute-start(f32[256]{0:T(256)S(1)} %get-tuple-element.153), channel_id=1, source_target_pairs={{0,1},{1,0},{2,3},{3,2},{4,5},{5,4},{6,7},{7,6},{8,9},{9,8},{10,11... | collective-permute-start | bytes 3080 | tf_op jit(solution)/shard_map/ppermute | solution.py:19
  107.6 2.1 %collective-permute-done.2 = f32[256]{0:T(256)S(1)} collective-permute-done((f32[256]{0:T(256)S(1)}, f32[256]{0:T(256)S(1)}, u32[]{:S(2)}, u32[]{:S(2)}) %collective-permute-start.2) | collective-permute-done | bytes 1056 | tf_op jit(solution)/shard_map/ppermute | solution.py:19
  109.7 0.8 multiply_convert_fusion.1
  (30 shorter events, 0.3 us)
Async XLA Ops:
  6.5 44.8 %copy-start = (bf16[4096,128]{1,0:T(8,128)(2,1)S(1)}, bf16[4096,128]{1,0:T(8,128)(2,1)}, u32[]{:S(2)}) copy-start(bf16[4096,128]{1,0:T(8,128)(2,1)} %param.17) | copy-start | bytes 3145732
  6.5 40.6 %all-gather.5.cloned.1.call-start = ((), (), s32[]{:S(2)}) async-start(), calls=%async_computation | async-start | bytes 2621440 | tf_op jit(solution)/shard_map/all_gather | solution.py:51
  7.3 85.1 %all-gather.7.cloned.1.call-start = ((), (), s32[]{:S(2)}) async-start(), calls=%async_computation.1 | async-start | bytes 2359296 | tf_op jit(solution)/shard_map/all_gather | solution.py:24
  47.1 4.2 %copy-start.1 = (bf16[256,4096]{1,0:T(8,128)(2,1)S(1)}, bf16[256,4096]{1,0:T(8,128)(2,1)}, u32[]{:S(2)}) copy-start(bf16[256,4096]{1,0:T(8,128)(2,1)} %all-gather.5.cloned.1.call-done) | copy-start | bytes 6291460
  51.4 2.3 %copy-start.3 = (f32[512]{0:T(512)S(1)}, f32[512]{0:T(512)}, u32[]{:S(2)}) copy-start(f32[512]{0:T(512)} %param.20) | copy-start | bytes 6148
  51.4 2.3 %copy-start.6 = (f32[128]{0:T(128)S(1)}, f32[128]{0:T(128)}, u32[]{:S(2)}) copy-start(f32[128]{0:T(128)} %param.21) | copy-start | bytes 1540
  52.1 2.4 %collective-permute-start = (bf16[3,640]{1,0:T(4,128)(2,1)S(1)}, bf16[3,640]{1,0:T(4,128)(2,1)S(1)}, u32[]{:S(2)}, u32[]{:S(2)}) collective-permute-start(bf16[3,640]{1,0:T(4,128)(2,1)S(1)} %pad_maximum_fusion), channel_id=1, source_target_pairs={{0,4},{4,8},{8,12},{12,16},{16,20},{20,24},{24,28},{1,5},{5,9},{9,... | collective-permute-start | bytes 11528 | tf_op jit(solution)/shard_map/ppermute | solution.py:13
  54.6 6.0 %copy-start.4 = (f32[8]{0:T(128)S(1)}, f32[8]{0:T(128)}, u32[]{:S(2)}) copy-start(f32[8]{0:T(128)} %param.24) | copy-start | bytes 100
  55.0 20.3 %copy-start.5 = (f32[8]{0:T(128)S(1)}, f32[8]{0:T(128)}, u32[]{:S(2)}) copy-start(f32[8]{0:T(128)} %param.23) | copy-start | bytes 100
  55.1 4.3 %collective-permute-start.1 = (bf16[256,128]{1,0:T(8,128)(2,1)S(1)}, bf16[256,128]{1,0:T(8,128)(2,1)S(1)}, u32[]{:S(2)}, u32[]{:S(2)}) collective-permute-start(bf16[256,128]{1,0:T(8,128)(2,1)S(1)} %slice.67), channel_id=1, source_target_pairs={{0,1},{1,0},{2,3},{3,2},{4,5},{5,4},{6,7},{7,6},{8,9},{9,8},{10,11... | collective-permute-start | bytes 196616 | tf_op jit(solution)/shard_map/ppermute | solution.py:19
  101.7 7.9 %copy-start.2 = (f32[512]{0:T(512)S(1)}, f32[512]{0:T(512)}, u32[]{:S(2)}) copy-start(f32[512]{0:T(512)} %param.25) | copy-start | bytes 6148
  106.0 3.6 %collective-permute-start.2 = (f32[256]{0:T(256)S(1)}, f32[256]{0:T(256)S(1)}, u32[]{:S(2)}, u32[]{:S(2)}) collective-permute-start(f32[256]{0:T(256)S(1)} %get-tuple-element.153), channel_id=1, source_target_pairs={{0,1},{1,0},{2,3},{3,2},{4,5},{5,4},{6,7},{7,6},{8,9},{9,8},{10,11... | collective-permute-start | bytes 3080 | tf_op jit(solution)/shard_map/ppermute | solution.py:19
Sparse Core Ops, SparseCore 0:
  9.2 37.8 all-gather.4
  60.6 31.6 all-gather.6
where the time goes:
time: 118 us; the launch traced here: 117 us
  waiting for transfers between devices  57.4 us (49%)
  blocking collectives  14.2 us (12%)
  between operations  13.6 us (12%)
  matrix products  12.7 us (11%)
  other arithmetic  12 us (10%)
  starting transfers between devices  4.68 us (4%)
  local copies, waits for them, and re-layouts  2.46 us (2%)
    all_gather x1, waiting for transfers between devices, local(): gathered = lax.all_gather(tokens, 'tp', axis=1, tiled=True)  35.9 us
    all_gather x1, waiting for transfers between devices, carried_in(): everything = jax.tree.map(lambda part: lax.all_gather(part, axis), shard)  15.3 us
    all_gather x1, blocking collectives, carried_in(): everything = jax.tree.map(lambda part: lax.all_gather(part, axis), shard)  14.2 us
    select_n x8, other arithmetic, lap(): return jax.tree.map(lambda a, b: jnp.where(reached, a, b), new, before)  8.42 us
    ppermute x2, waiting for transfers between devices, partner(): return lax.ppermute(value, axis, pairs)  4.73 us
    dot_general x1, matrix products, local(): gate_sum = jnp.dot(gathered, w_z, preferred_element_type=jnp.float32)  4.28 us
    dot_general x1, matrix products, local(): x_sum = jnp.dot(gathered, w_x, preferred_element_type=jnp.float32)  4.21 us
    ppermute x2, starting transfers between devices, partner(): return lax.ppermute(value, axis, pairs)  3.07 us
  transfers between devices with their start and end apart: 5, of which 5 were waited for; matrix products, arithmetic and copies ran while one was open for 5% of the time, Pallas kernels for 0%

commit v1 on v0

--- a/solution.py
+++ b/solution.py
@@ -48,7 +48,14 @@
     bc_width = w_bc.shape[1]
     heads_local = head_step.shape[0]
     head_dim = x_width // heads_local
-    gathered = lax.all_gather(tokens, "tp", axis=1, tiled=True)
+    ways, here, step = (lax.axis_size("tp"), lax.axis_index("tp"), tokens.shape[1])
+    line, have = (tokens, 1)
+    while have < ways:
+        line = jnp.concatenate(
+            [line, lax.ppermute(line, "tp", [(d, (d - have) % ways) for d in range(ways)])], axis=1
+        )
+        have = 2 * have
+    gathered = jnp.roll(line, here * step, axis=1)
     gate_sum = jnp.dot(gathered, w_z, preferred_element_type=jnp.float32)
     x_sum = jnp.dot(gathered, w_x, preferred_element_type=jnp.float32)
     bc_sum = jnp.dot(gathered, w_bc, preferred_element_type=jnp.float32)

time: 118 us -> 125 us (1.059)
  waiting for transfers between devices: 57.4 us -> 49.4 us
  local copies, waits for them, and re-layouts: 2.46 us -> 9.11 us
  starting transfers between devices: 4.68 us -> 10.6 us
  other arithmetic: 12 us -> 14.1 us
    all_gather x1 -> x0, waiting for transfers between devices: 35.9 us -> none  [local(): gathered = lax.all_gather(tokens, 'tp', axis=1, tiled=True)]
    ppermute x0 -> x2, waiting for transfers between devices: none -> 27.6 us  [local(): lax.ppermute(line, 'tp', [(d, (d - have) % ways) for d in range(ways)])]
    unnamed x15 -> x22, local copies, waits for them, and re-layouts: 0.74 us -> 6.34 us
    ppermute x0 -> x2, starting transfers between devices: none -> 5.37 us  [local(): lax.ppermute(line, 'tp', [(d, (d - have) % ways) for d in range(ways)])]
    concatenate x0 -> x1, other arithmetic: none -> 2.1 us  [local(): jnp.concatenate([line, lax.ppermute(line, 'tp', [(d, (d - have) % ways) f...]
    dot_general x1, matrix products: 0.72 us -> 2.29 us  [local(): bc_sum = jnp.dot(gathered, w_bc, preferred_element_type=jnp.float32)]
    all_gather x1, waiting for transfers between devices: 15.3 us -> 16.8 us  [carried_in(): everything = jax.tree.map(lambda part: lax.all_gather(part, axis), shard)]
    dot_general x1, matrix products: 4.21 us -> 2.89 us  [local(): x_sum = jnp.dot(gathered, w_x, preferred_element_type=jnp.float32)]
  transfers between devices with their start and end apart: 5 -> 6, of which waited for: 5 -> 6; matrix products, arithmetic and copies ran while one was open for 5% -> 7% of each run, Pallas kernels for 0% -> 0%
where the time goes in v1:
time: 125 us
  waiting for transfers between devices  49.4 us (40%)
  blocking collectives  14.8 us (12%)
  other arithmetic  14.1 us (11%)
  between operations  13.6 us (11%)
  matrix products  12.9 us (10%)
  starting transfers between devices  10.6 us (8%)
  local copies, waits for them, and re-layouts  9.11 us (7%)
    ppermute x2, waiting for transfers between devices, local(): lax.ppermute(line, 'tp', [(d, (d - have) % ways) for d in range(ways)])  27.6 us
    all_gather x1, waiting for transfers between devices, carried_in(): everything = jax.tree.map(lambda part: lax.all_gather(part, axis), shard)  16.8 us
    all_gather x1, blocking collectives, carried_in(): everything = jax.tree.map(lambda part: lax.all_gather(part, axis), shard)  14.8 us
    select_n x8, other arithmetic, lap(): return jax.tree.map(lambda a, b: jnp.where(reached, a, b), new, before)  8.42 us
    unnamed x22, local copies, waits for them, and re-layouts  6.34 us
    ppermute x2, starting transfers between devices, local(): lax.ppermute(line, 'tp', [(d, (d - have) % ways) for d in range(ways)])  5.37 us
    dot_general x1, matrix products, local(): gate_sum = jnp.dot(gathered, w_z, preferred_element_type=jnp.float32)  4.27 us
    ppermute x2, waiting for transfers between devices, partner(): return lax.ppermute(value, axis, pairs)  4.18 us
  transfers between devices with their start and end apart: 6, of which 6 were waited for; matrix products, arithmetic and copies ran while one was open for 7% of the time, Pallas kernels for 0%

profile of v1, /device:TPU:0, one launch (start us, length us, event | category | flops | bytes accessed | tf_op | source)
XLA Modules:
  0.0 124.7 jit_solution(12044334286129738081)
XLA Ops:
  6.5 3.9 %collective-permute-start = (bf16[256,1024]{1,0:T(8,128)(2,1)}, bf16[256,1024]{1,0:T(8,128)(2,1)S(1)}, u32[]{:S(2)}, u32[]{:S(2)}) collective-permute-start(bf16[256,1024]{1,0:T(8,128)(2,1)} %param.14), channel_id=1, source_target_pairs={{0,3},{1,0},{2,1},{3,2},{4,7},{5,4},{6,5},{7,6},{8,11},{9,8},{10,9... | collective-permute-start | bytes 1572872 | tf_op jit(solution)/shard_map/ppermute | solution.py:55
  10.5 1.2 reduce-window.6
  11.7 0.7 constant_dynamic-update-slice_fusion.1
  12.4 0.7 constant_dynamic-update-slice_fusion
  13.1 1.9 %constant_dynamic-update-slice_fusion.7 = bf16[256,8192]{1,0:T(8,128)(2,1)} fusion(bf16[256,1024]{1,0:T(8,128)(2,1)} %param.14), kind=kLoop, calls=%fused_computation.63 | loop fusion | bytes 1048576
  15.1 6.9 %collective-permute-done = bf16[256,1024]{1,0:T(8,128)(2,1)S(1)} collective-permute-done((bf16[256,1024]{1,0:T(8,128)(2,1)}, bf16[256,1024]{1,0:T(8,128)(2,1)S(1)}, u32[]{:S(2)}, u32[]{:S(2)}) %collective-permute-start) | collective-permute-done | bytes 524320 | tf_op jit(solution)/shard_map/ppermute | solution.py:55
  22.0 2.1 %pad_maximum_fusion = bf16[256,2048]{1,0:T(8,128)(2,1)} fusion(bf16[256,1024]{1,0:T(8,128)(2,1)S(1)} %collective-permute-done, bf16[256,1024]{1,0:T(8,128)(2,1)} %param.14), kind=kLoop, calls=%fused_computation.25 | loop fusion | flops 2097152 | bytes 2097152 | tf_op jit(solution)/shard_map/concatenate | solution.py:54
  24.1 1.4 %collective-permute-start.1 = (bf16[256,2048]{1,0:T(8,128)(2,1)}, bf16[256,2048]{1,0:T(8,128)(2,1)S(1)}, u32[]{:S(2)}, u32[]{:S(2)}) collective-permute-start(bf16[256,2048]{1,0:T(8,128)(2,1)} %pad_maximum_fusion), channel_id=1, source_target_pairs={{0,2},{1,3},{2,0},{3,1},{4,6},{5,7},{6,4},{7,5},{8,10},{9,11},{10,... | collective-permute-start | bytes 3145736 | tf_op jit(solution)/shard_map/ppermute | solution.py:55
  25.5 0.2 slice_reduce_fusion
  25.7 0.1 exponential_bitcast_fusion.1
  25.8 0.2 slice_reduce_fusion.5
  26.0 0.7 multiply_bitcast_fusion
  26.7 0.9 constant_dynamic-update-slice_fusion.6
  27.6 20.7 %collective-permute-done.1 = bf16[256,2048]{1,0:T(8,128)(2,1)S(1)} collective-permute-done((bf16[256,2048]{1,0:T(8,128)(2,1)}, bf16[256,2048]{1,0:T(8,128)(2,1)S(1)}, u32[]{:S(2)}, u32[]{:S(2)}) %collective-permute-start.1) | collective-permute-done | bytes 1048608 | tf_op jit(solution)/shard_map/ppermute | solution.py:55
  48.3 1.1 constant_dynamic-update-slice_fusion.5
  49.4 0.9 constant_dynamic-update-slice_fusion.4
  50.2 0.9 constant_dynamic-update-slice_fusion.3
  51.1 1.0 constant_dynamic-update-slice_fusion.2
  52.2 2.3 %fusion.28 = bf16[256,128]{1,0:T(8,128)(2,1)S(1)} fusion(bf16[4096,128]{1,0:T(8,128)(2,1)S(1)} %copy-done, bf16[256,8192]{1,0:T(8,128)(2,1)} %constant_dynamic-update-slice_fusion.2, s32[]{:T(128)S(6)} %select_n.69), kind=kOutput, calls=%fused_computation.24 | convolution fusion | flops 268468224 | bytes 3211268 | tf_op jit(solution)/shard_map/dot_general | solution.py:61
  54.5 2.9 %fusion.19 = bf16[256,512]{1,0:T(8,128)(2,1)S(1)} fusion(bf16[4096,512]{1,0:T(8,128)(2,1)S(1)} %copy-done.7, bf16[256,8192]{1,0:T(8,128)(2,1)} %constant_dynamic-update-slice_fusion.2, s32[]{:T(128)S(6)} %select_n.69), kind=kOutput, calls=%fused_computation.20 | convolution fusion | flops 1073872896 | bytes 6553604 | tf_op jit(solution)/shard_map/dot_general | solution.py:60
  57.4 1.3 %collective-permute-start.2 = (bf16[3,640]{1,0:T(4,128)(2,1)S(1)}, bf16[3,640]{1,0:T(4,128)(2,1)S(1)}, u32[]{:S(2)}, u32[]{:S(2)}) collective-permute-start(bf16[3,640]{1,0:T(4,128)(2,1)S(1)} %pad_maximum_fusion.1), channel_id=1, source_target_pairs={{0,4},{4,8},{8,12},{12,16},{16,20},{20,24},{24,28},{1,5},{5,9},{9,... | collective-permute-start | bytes 11528 | tf_op jit(solution)/shard_map/ppermute | solution.py:13
  58.8 0.8 collective-permute-done.2
  59.6 0.4 multiply_convert_fusion
  60.1 2.4 %collective-permute-start.3 = (bf16[256,128]{1,0:T(8,128)(2,1)S(1)}, bf16[256,128]{1,0:T(8,128)(2,1)S(1)}, u32[]{:S(2)}, u32[]{:S(2)}) collective-permute-start(bf16[256,128]{1,0:T(8,128)(2,1)S(1)} %slice.67), channel_id=1, source_target_pairs={{0,1},{1,0},{2,3},{3,2},{4,5},{5,4},{6,7},{7,6},{8,9},{9,8},{10,11... | collective-permute-start | bytes 196616 | tf_op jit(solution)/shard_map/ppermute | solution.py:19
  62.5 0.1 copy.28
  62.6 2.1 %collective-permute-done.3 = bf16[256,128]{1,0:T(8,128)(2,1)S(1)} collective-permute-done((bf16[256,128]{1,0:T(8,128)(2,1)S(1)}, bf16[256,128]{1,0:T(8,128)(2,1)S(1)}, u32[]{:S(2)}, u32[]{:S(2)}) %collective-permute-start.3) | collective-permute-done | bytes 65568 | tf_op jit(solution)/shard_map/ppermute | solution.py:19
  64.7 1.1 convolution_add_fusion
  65.8 0.1 copy.29
  66.0 0.1 mul.202
  66.1 14.8 %all-gather = f32[8,1,8]{2,1,0:T(1,128)S(1)} all-gather(f32[1,1,8]{2,1,0:T(1,128)S(1)} %copy.29), channel_id=2, replica_groups=mesh['ctx'=8,'tp'=4] {'ctx'}, dimensions={0}, use_global_device_ids=true | all-gather | bytes 288 | tf_op jit(solution)/shard_map/all_gather | solution.py:24
  81.0 0.2 fusion.50
  81.2 1.8 %fusion.14 = f32[1,256,8,64]{1,3,2,0:T(8,128)S(1)} fusion(bf16[256,8,64]{0,2,1:T(8,128)(2,1)S(1)} %bitcast.66, f32[8]{0:T(128)S(1)} %copy-done.5, f32[256,256]{1,0:T(8,128)S(1)} %fusion.50, f32[256,8]{0,1:T(8,128)S(1)} %fusion.51, pred[256,256]{1,0:T(8,128)(4,1)S(1)} %iota_compare_fusion), kind=kOutput, calls=%fused_computation.16 | convolution fusion | flops 405274624 | bytes 1122336 | tf_op jit(solution)/shard_map/cijh,cjhp->cihp/dot_general | solution.py:93
  83.0 16.8 %all-gather.4.cloned.1.call-done = f32[64,64,128]{2,1,0:T(8,128)} async-done(((f32[8,64,128]{2,1,0:T(8,128)}), f32[64,64,128]{2,1,0:T(8,128)}) %all-gather.4.cloned.1.call-update) | async-done | bytes 2097168 | tf_op jit(solution)/shard_map/all_gather | solution.py:24
  99.7 8.7 %while.9 = (s32[]{:T(128)}, f32[8,64,128]{2,1,0:T(8,128)S(1)}, s32[]{:T(128)}, f32[8,8]{1,0:T(8,128)S(1)}, f32[8,8,64,128]{3,2,1,0:T(8,128)}, /*index=5*/s32[]{:T(128)}, s32[]{:T(128)}) while((s32[]{:T(128)}, f32[8,64,128]{2,1,0:T(8,128)S(1)}, s32[]{:T(128)}, f32[8,8]{1,0:T(8,128)S(1)}, f32[8,8,64,128]{3,2,1,0:T(8,128)}, ...), condition=%wide.region_3.4_spmd.clone, body=%wide.region_2.3_spmd.clone.sunk | while | flops 262148 | bytes 786641 | solution.py:36
  99.8 1.1 fusion.66
  100.9 1.1 fusion.66
  102.0 1.1 fusion.66
  103.0 1.1 fusion.66
  104.1 1.1 fusion.66
  105.2 1.1 fusion.66
  106.3 1.1 fusion.66
  107.4 1.1 fusion.66
  108.5 0.4 fusion.18
  108.9 0.2 copy.30
  109.1 4.3 %multiply_reduce_fusion = (f32[256]{0:T(256)S(1)}, f32[256,512]{1,0:T(8,128)S(1)}) fusion(bf16[4096,512]{1,0:T(8,128)(2,1)} %param.15, bf16[256,8192]{1,0:T(8,128)(2,1)} %constant_dynamic-update-slice_fusion.2, s32[]{:T(128)S(6)} %select_n.69, f32[256,512]{1,0:T(8,128)S(1)} %copy.30, bf16[256,640]{1,0:T(8,128)(2,1)S(1)} %multiply_convert_fusion, ...), kind=kOutput, calls=%fused_computation.42 | convolution fusion | flops 1075314432 | bytes 7605252 | tf_op jit(solution)/shard_map/dot_general | solution.py:59
  113.4 1.5 %collective-permute-start.4 = (f32[256]{0:T(256)S(1)}, f32[256]{0:T(256)S(1)}, u32[]{:S(2)}, u32[]{:S(2)}) collective-permute-start(f32[256]{0:T(256)S(1)} %get-tuple-element.153), channel_id=1, source_target_pairs={{0,1},{1,0},{2,3},{3,2},{4,5},{5,4},{6,7},{7,6},{8,9},{9,8},{10,11... | collective-permute-start | bytes 3080 | tf_op jit(solution)/shard_map/ppermute | solution.py:19
  114.9 2.1 %collective-permute-done.4 = f32[256]{0:T(256)S(1)} collective-permute-done((f32[256]{0:T(256)S(1)}, f32[256]{0:T(256)S(1)}, u32[]{:S(2)}, u32[]{:S(2)}) %collective-permute-start.4) | collective-permute-done | bytes 1056 | tf_op jit(solution)/shard_map/ppermute | solution.py:19
  117.1 0.8 multiply_convert_fusion.1
  (40 shorter events, 0.5 us)
Async XLA Ops:
  6.5 45.6 %copy-start = (bf16[4096,128]{1,0:T(8,128)(2,1)S(1)}, bf16[4096,128]{1,0:T(8,128)(2,1)}, u32[]{:S(2)}) copy-start(bf16[4096,128]{1,0:T(8,128)(2,1)} %param.17) | copy-start | bytes 3145732
  6.5 42.8 %copy-start.1 = (bf16[256,1024]{1,0:T(8,128)(2,1)S(1)}, bf16[256,1024]{1,0:T(8,128)(2,1)}, u32[]{:S(2)}) copy-start(bf16[256,1024]{1,0:T(8,128)(2,1)} %param.14) | copy-start | bytes 1572868
  6.5 93.2 %all-gather.4.cloned.1.call-start = ((), (), s32[]{:S(2)}) async-start(), calls=%async_computation | async-start | bytes 2359296 | tf_op jit(solution)/shard_map/all_gather | solution.py:24
  6.5 15.4 %collective-permute-start = (bf16[256,1024]{1,0:T(8,128)(2,1)}, bf16[256,1024]{1,0:T(8,128)(2,1)S(1)}, u32[]{:S(2)}, u32[]{:S(2)}) collective-permute-start(bf16[256,1024]{1,0:T(8,128)(2,1)} %param.14), channel_id=1, source_target_pairs={{0,3},{1,0},{2,1},{3,2},{4,7},{5,4},{6,5},{7,6},{8,11},{9,8},{10,9... | collective-permute-start | bytes 1572872 | tf_op jit(solution)/shard_map/ppermute | solution.py:55
  24.1 24.3 %collective-permute-start.1 = (bf16[256,2048]{1,0:T(8,128)(2,1)}, bf16[256,2048]{1,0:T(8,128)(2,1)S(1)}, u32[]{:S(2)}, u32[]{:S(2)}) collective-permute-start(bf16[256,2048]{1,0:T(8,128)(2,1)} %pad_maximum_fusion), channel_id=1, source_target_pairs={{0,2},{1,3},{2,0},{3,1},{4,6},{5,7},{6,4},{7,5},{8,10},{9,11},{10,... | collective-permute-start | bytes 3145736 | tf_op jit(solution)/shard_map/ppermute | solution.py:55
  49.4 5.1 %copy-start.7 = (bf16[4096,512]{1,0:T(8,128)(2,1)S(1)}, bf16[4096,512]{1,0:T(8,128)(2,1)}, u32[]{:S(2)}) copy-start(bf16[4096,512]{1,0:T(8,128)(2,1)} %param.16) | copy-start | bytes 12582916
  54.5 4.3 %copy-start.3 = (f32[512]{0:T(512)S(1)}, f32[512]{0:T(512)}, u32[]{:S(2)}) copy-start(f32[512]{0:T(512)} %param.20) | copy-start | bytes 6148
  54.5 4.3 %copy-start.6 = (f32[128]{0:T(128)S(1)}, f32[128]{0:T(128)}, u32[]{:S(2)}) copy-start(f32[128]{0:T(128)} %param.21) | copy-start | bytes 1540
  57.4 8.5 %copy-start.4 = (f32[8]{0:T(128)S(1)}, f32[8]{0:T(128)}, u32[]{:S(2)}) copy-start(f32[8]{0:T(128)} %param.24) | copy-start | bytes 100
  57.4 23.8 %copy-start.5 = (f32[8]{0:T(128)S(1)}, f32[8]{0:T(128)}, u32[]{:S(2)}) copy-start(f32[8]{0:T(128)} %param.23) | copy-start | bytes 100
  57.4 2.1 %collective-permute-start.2 = (bf16[3,640]{1,0:T(4,128)(2,1)S(1)}, bf16[3,640]{1,0:T(4,128)(2,1)S(1)}, u32[]{:S(2)}, u32[]{:S(2)}) collective-permute-start(bf16[3,640]{1,0:T(4,128)(2,1)S(1)} %pad_maximum_fusion.1), channel_id=1, source_target_pairs={{0,4},{4,8},{8,12},{12,16},{16,20},{20,24},{24,28},{1,5},{5,9},{9,... | collective-permute-start | bytes 11528 | tf_op jit(solution)/shard_map/ppermute | solution.py:13
  60.1 4.6 %collective-permute-start.3 = (bf16[256,128]{1,0:T(8,128)(2,1)S(1)}, bf16[256,128]{1,0:T(8,128)(2,1)S(1)}, u32[]{:S(2)}, u32[]{:S(2)}) collective-permute-start(bf16[256,128]{1,0:T(8,128)(2,1)S(1)} %slice.67), channel_id=1, source_target_pairs={{0,1},{1,0},{2,3},{3,2},{4,5},{5,4},{6,7},{7,6},{8,9},{9,8},{10,11... | collective-permute-start | bytes 196616 | tf_op jit(solution)/shard_map/ppermute | solution.py:19
  109.1 7.9 %copy-start.2 = (f32[512]{0:T(512)S(1)}, f32[512]{0:T(512)}, u32[]{:S(2)}) copy-start(f32[512]{0:T(512)} %param.25) | copy-start | bytes 6148
  113.4 3.6 %collective-permute-start.4 = (f32[256]{0:T(256)S(1)}, f32[256]{0:T(256)S(1)}, u32[]{:S(2)}, u32[]{:S(2)}) collective-permute-start(f32[256]{0:T(256)S(1)} %get-tuple-element.153), channel_id=1, source_target_pairs={{0,1},{1,0},{2,3},{3,2},{4,5},{5,4},{6,7},{7,6},{8,9},{9,8},{10,11... | collective-permute-start | bytes 3080 | tf_op jit(solution)/shard_map/ppermute | solution.py:19
Sparse Core Ops, SparseCore 0:
  66.0 33.7 all-gather.3
